TPU v7x, 256 devices: a whole 4x4x8 slice. The times are simulated.
256 devices in a mesh: tm: 64 (over y, z, core), chan: 4 (over x).
Axes of the slice: x: 4, y: 4, z: 8, core: 2. Of those that a mesh axis runs over, the one named last changes fastest.
Arguments:
- signals: bfloat16 [262144, 2048], P('tm', 'chan')
- channel_node: int32 [2048], P('chan'), may hold values from 0 to 127, as said below
- lag_offsets: int32 [8], replicated, may hold values from 0 to 512, as said below
Outputs:
- r_factor: float32 [1024, 1024], replicated
Inputs may be any that keep to these rules, and one draw needn't show every extreme that they name: `channel_node`: every node is named by exactly 16 channels; which channels, and so which channel groups, is drawn. `lag_offsets`: strictly increasing; the first is 0 and the last is 512.
All inputs are finite; a program needn't handle non-finite values.
Results may differ from a plain program's by a relative error of at most 0.0003.
Values sent between devices are 32-bit elements; how exact they have to be, the bound alone decides.
A program may use at most 64 MiB of HBM per device.

v0:
```python
import math
import jax
import jax.numpy as jnp
from jax import lax
from jax.sharding import PartitionSpec as P

NODES = 128
CH = 2048
MAXLAG = 512


def from_behind(value, axis, steps):
    count = lax.axis_size(axis)
    leading, last = (max(0, -steps), min(count, count - steps))
    return lax.ppermute(value, axis, [(source, source + steps) for source in range(leading, last)])


def on_device(signals, channel_node, lag_offsets):
    group_count = lax.axis_size("chan")
    lag_count = lag_offsets.shape[0]
    group_width = NODES // group_count
    onehot = (channel_node[:, None] == jnp.arange(NODES, dtype=jnp.int32)[None, :]).astype(
        jnp.bfloat16
    )
    partial_value = jnp.dot(signals, onehot, preferred_element_type=jnp.float32)
    node_scale = 1.0 / math.sqrt(CH // NODES)
    node_share = (
        lax.psum_scatter(partial_value, "chan", scatter_dimension=1, tiled=True) * node_scale
    )
    rim_rows = from_behind(node_share[:MAXLAG], "tm", -1)
    extended = jnp.concatenate([node_share, rim_rows], axis=0)
    time_rows = node_share.shape[0]
    columns = []
    for lag_index in range(lag_count):
        columns.append(
            lax.dynamic_slice(
                extended, (lag_offsets[lag_index], jnp.int32(0)), (time_rows, group_width)
            )
        )
    panel = jnp.concatenate(columns, axis=1)
    hankel = lax.all_to_all(panel, "chan", split_axis=0, concat_axis=1, tiled=True)
    row_total = hankel.shape[0] * lax.axis_size("tm") * group_count
    local_gram = lax.dot_general(
        hankel,
        hankel,
        (((0,), (0,)), ((), ())),
        precision=lax.Precision.HIGHEST,
        preferred_element_type=jnp.float32,
    )
    gram_matrix = lax.psum(local_gram, ("tm", "chan"))
    return jnp.linalg.cholesky(gram_matrix / row_total).T


def solution(mesh):
    in_specs = (P("tm", "chan"), P("chan"), P())
    out_specs = P()
    return jax.shard_map(
        on_device, mesh=mesh, in_specs=in_specs, out_specs=out_specs, check_vma=False
    )
```

profile of v0, /device:TPU:2, one launch (start us, length us, event | category | flops | bytes accessed | tf_op | source)
XLA Modules:
  0.0 642.1 jit_solution(7835683541833374549)
XLA Ops:
  6.5 5.2 convolution_bitcast_fusion
  11.8 34.0 %reduce-scatter.2.cloned.1.call-done = f32[4096,32]{0,1:T(8,128)} async-done(((f32[4096,128]{0,1:T(8,128)}), f32[4096,32]{0,1:T(8,128)}) %reduce-scatter.2.cloned.1.call-update) | async-done | bytes 524304 | tf_op jit(solution)/shard_map/reduce_scatter | solution.py:28
  45.8 1.1 broadcast_multiply_fusion.1
  46.9 1.3 collective-permute-start
  48.2 0.7 fusion.47
  67.2 53.2 %all_to_all.19 = f32[4,1024,256]{1,2,0:T(8,128)S(1)} all-to-all(f32[4,1024,256]{1,2,0:T(8,128)S(1)} %bitcast.64), channel_id=1, replica_groups=mesh['tm'=64,'chan'=4] {'chan'}, dimensions={0} | all-to-all | bytes 8388608 | tf_op jit(solution)/shard_map/all_to_all | solution.py:41
  120.4 14.9 %fusion.48 = f32[1024,1024]{0,1:T(8,128)} fusion(f32[1024,1024]{0,1:T(8,128)S(1)} %bitcast.66), kind=kOutput, calls=%fused_computation.117 | convolution fusion | flops 12884901888 | bytes 8388608 | tf_op jit(solution)/shard_map/dot_general | solution.py:43
  135.3 269.4 %all-reduce.3.cloned.1.call-done = f32[1024,1024]{0,1:T(8,128)} async-done(((f32[1024,1024]{0,1:T(8,128)}), f32[1024,1024]{0,1:T(8,128)}) %all-reduce.3.cloned.1.call-update) | async-done | bytes 4194320 | tf_op jit(solution)/shard_map/psum | solution.py:50
  404.7 5.0 broadcast_multiply_fusion
  409.7 5.8 copy.9
  415.6 4.4 fusion
  420.1 1.9 copy-done
  422.0 11.7 %cholesky.223 = f32[128,128]{1,0:T(8,128)S(1)} custom-call(f32[128,128]{1,0:T(8,128)S(1)} %cholesky.580), custom_call_target="Cholesky" | custom-call | tf_op jit(solution)/shard_map/jit(cholesky)/cholesky | solution.py:51
  433.7 9.8 %custom-call.59 = f32[1,128,128]{1,2,0:T(8,128)S(1)} custom-call(f32[1,128,128]{2,1,0:T(8,128)S(1)} %get-tuple-element.26), custom_call_target="InvertDiagBlocksLowerTriangular" | custom-call | tf_op jit(solution)/shard_map/jit(cholesky)/cholesky | solution.py:51
  443.6 2.5 cholesky.255
  446.1 2.3 constant_dynamic-update-slice_fusion
  448.4 1.5 convolution_subtract_fusion
  450.0 11.9 %cholesky.244 = f32[128,128]{1,0:T(8,128)S(1)} custom-call(f32[128,128]{1,0:T(8,128)S(1)} %cholesky.584), custom_call_target="Cholesky" | custom-call | tf_op jit(solution)/shard_map/jit(cholesky)/cholesky | solution.py:51
  462.5 9.8 %custom-call.60 = f32[1,128,128]{1,2,0:T(8,128)S(1)} custom-call(f32[1,128,128]{2,1,0:T(8,128)S(1)} %get-tuple-element.23), custom_call_target="InvertDiagBlocksLowerTriangular" | custom-call | tf_op jit(solution)/shard_map/jit(cholesky)/cholesky | solution.py:51
  472.3 1.2 convolution_dynamic-update-slice_fusion
  473.5 2.1 convolution_subtract_fusion.1
  475.6 11.7 %cholesky.468 = f32[128,128]{1,0:T(8,128)S(1)} custom-call(f32[128,128]{1,0:T(8,128)S(1)} %cholesky.589), custom_call_target="Cholesky" | custom-call | tf_op jit(solution)/shard_map/jit(cholesky)/cholesky | solution.py:51
  488.6 9.8 %custom-call.61 = f32[1,128,128]{1,2,0:T(8,128)S(1)} custom-call(f32[1,128,128]{2,1,0:T(8,128)S(1)} %get-tuple-element.20), custom_call_target="InvertDiagBlocksLowerTriangular" | custom-call | tf_op jit(solution)/shard_map/jit(cholesky)/cholesky | solution.py:51
  498.4 1.1 convolution_dynamic-update-slice_fusion.1
  499.6 2.3 convolution_subtract_fusion.2
  501.9 11.9 %cholesky.487 = f32[128,128]{1,0:T(8,128)S(1)} custom-call(f32[128,128]{1,0:T(8,128)S(1)} %cholesky.594), custom_call_target="Cholesky" | custom-call | tf_op jit(solution)/shard_map/jit(cholesky)/cholesky | solution.py:51
  514.5 0.7 compare_reduce_fusion.4
  515.1 9.8 %custom-call.62 = f32[1,128,128]{1,2,0:T(8,128)S(1)} custom-call(f32[1,128,128]{2,1,0:T(8,128)S(1)} %get-tuple-element.17), custom_call_target="InvertDiagBlocksLowerTriangular" | custom-call | tf_op jit(solution)/shard_map/jit(cholesky)/cholesky | solution.py:51
  525.0 1.1 convolution_dynamic-update-slice_fusion.2
  526.0 2.4 convolution_subtract_fusion.3
  528.4 11.7 %cholesky.506 = f32[128,128]{1,0:T(8,128)S(1)} custom-call(f32[128,128]{1,0:T(8,128)S(1)} %cholesky.599), custom_call_target="Cholesky" | custom-call | tf_op jit(solution)/shard_map/jit(cholesky)/cholesky | solution.py:51
  540.8 0.7 compare_reduce_fusion.3
  541.5 10.2 %custom-call.63 = f32[1,128,128]{1,2,0:T(8,128)S(1)} custom-call(f32[1,128,128]{2,1,0:T(8,128)S(1)} %get-tuple-element.14), custom_call_target="InvertDiagBlocksLowerTriangular" | custom-call | tf_op jit(solution)/shard_map/jit(cholesky)/cholesky | solution.py:51
  551.7 1.0 convolution_dynamic-update-slice_fusion.3
  552.7 2.3 convolution_subtract_fusion.4
  555.0 11.7 %cholesky.526 = f32[128,128]{1,0:T(8,128)S(1)} custom-call(f32[128,128]{1,0:T(8,128)S(1)} %cholesky.604), custom_call_target="Cholesky" | custom-call | tf_op jit(solution)/shard_map/jit(cholesky)/cholesky | solution.py:51
  568.0 9.8 %custom-call.64 = f32[1,128,128]{1,2,0:T(8,128)S(1)} custom-call(f32[1,128,128]{2,1,0:T(8,128)S(1)} %get-tuple-element.11), custom_call_target="InvertDiagBlocksLowerTriangular" | custom-call | tf_op jit(solution)/shard_map/jit(cholesky)/cholesky | solution.py:51
  577.8 0.9 convolution_dynamic-update-slice_fusion.4
  578.7 2.0 convolution_subtract_fusion.5
  580.7 11.9 %cholesky.546 = f32[128,128]{1,0:T(8,128)S(1)} custom-call(f32[128,128]{1,0:T(8,128)S(1)} %cholesky.609), custom_call_target="Cholesky" | custom-call | tf_op jit(solution)/shard_map/jit(cholesky)/cholesky | solution.py:51
  593.9 9.8 %custom-call.65 = f32[1,128,128]{1,2,0:T(8,128)S(1)} custom-call(f32[1,128,128]{2,1,0:T(8,128)S(1)} %get-tuple-element.8), custom_call_target="InvertDiagBlocksLowerTriangular" | custom-call | tf_op jit(solution)/shard_map/jit(cholesky)/cholesky | solution.py:51
  603.7 0.8 convolution_dynamic-update-slice_fusion.5
  604.5 1.8 convolution_subtract_fusion.6
  606.3 11.7 %cholesky.564 = f32[128,128]{1,0:T(8,128)S(1)} custom-call(f32[128,128]{1,0:T(8,128)S(1)} %convolution_subtract_fusion.6), custom_call_target="Cholesky" | custom-call | tf_op jit(solution)/shard_map/jit(cholesky)/cholesky | solution.py:51
  618.7 0.7 compare_reduce_fusion
  619.4 0.7 compare_reduce_fusion.6
  625.0 4.8 select_bitcast_fusion
  629.7 5.3 copy.10
  (36 shorter events, 9.9 us)
Async XLA Ops:
  6.5 41.7 %copy-start.1 = (s32[8]{0:T(128)S(1)}, s32[8]{0:T(128)}, u32[]{:S(2)}) copy-start(s32[8]{0:T(128)} %param.5) | copy-start | bytes 100
  6.5 39.3 %reduce-scatter.2.cloned.1.call-start = ((), (), s32[]{:S(2)}) async-start(), calls=%async_computation.2 | async-start | bytes 2621440 | tf_op jit(solution)/shard_map/reduce_scatter | solution.py:28
  11.7 393.0 %all-reduce.3.cloned.1.call-start = ((), (), s32[]{:S(2)}) async-start(), calls=%async_computation.3 | async-start | bytes 8388608 | tf_op jit(solution)/shard_map/psum | solution.py:50
  46.9 16.8 %collective-permute-start = (f32[512,32]{0,1:T(8,128)S(1)}, f32[512,32]{0,1:T(8,128)S(1)}, u32[]{:S(2)}, u32[]{:S(2)}) collective-permute-start(f32[512,32]{0,1:T(8,128)S(1)} %slice.213), channel_id=1, source_target_pairs={{4,0},{8,4},{12,8},{16,12},{20,16},{24,20},{28,24},{32,28},{36,32}... | collective-permute-start | bytes 196616 | tf_op jit(solution)/shard_map/ppermute | solution.py:15
  420.1 1.9 copy-start
Sparse Core Ops, SparseCore 0:
  11.9 33.9 reduce-scatter.1
  135.4 269.2 all-reduce.2
where the time goes:
time: 647 us; the launch traced here: 642 us
  waiting for transfers between devices  303 us (47%)
  other arithmetic  190 us (29%)
  blocking collectives  53.2 us (8%)
  matrix products  43 us (7%)
  between operations  33.6 us (5%)
  local copies, waits for them, and re-layouts  16.9 us (3%)
    psum x1, waiting for transfers between devices, on_device(): gram_matrix = lax.psum(local_gram, ('tm', 'chan'))  269 us
    another operation x30, other arithmetic, on_device(): return jnp.linalg.cholesky(gram_matrix / row_total).T  172 us
    all_to_all x1, blocking collectives, on_device(): lax.all_to_all(panel, 'chan', split_axis=0, concat_axis=1, tiled=True)  53.2 us
    reduce_scatter x1, waiting for transfers between devices, on_device(): lax.psum_scatter(partial_value, 'chan', scatter_dimension=1, tiled=True)  34 us
    another operation x14, matrix products, on_device(): return jnp.linalg.cholesky(gram_matrix / row_total).T  22.9 us
    dot_general x1, matrix products, on_device(): lax.dot_general(hankel, hankel, (((0,), (0,)), ((), ())), precision=lax.P...  14.9 us
  transfers between devices with their start and end apart: 3, of which 2 were waited for; matrix products, arithmetic and copies ran while one was open for 0% of the time, Pallas kernels for 0%

commit v1 on v0

--- a/solution.py
+++ b/solution.py
@@ -47,7 +47,7 @@
         precision=lax.Precision.HIGHEST,
         preferred_element_type=jnp.float32,
     )
-    gram_matrix = lax.psum(local_gram, ("tm", "chan"))
+    gram_matrix = lax.psum(lax.psum(local_gram, "chan"), "tm")
     return jnp.linalg.cholesky(gram_matrix / row_total).T
 
 

time: 647 us -> 675 us (1.043)
  waiting for transfers between devices: 303 us -> 332 us
    psum x1 -> x2, waiting for transfers between devices: 269 us -> 298 us  [on_device(): gram_matrix = lax.psum(lax.psum(local_gram, 'chan'), 'tm')]
  transfers between devices with their start and end apart: 3 -> 4, of which waited for: 2 -> 3; matrix products, arithmetic and copies ran while one was open for 0% -> 0% of each run, Pallas kernels for 0% -> 0%
where the time goes in v1:
time: 675 us; the launch traced here: 670 us
  waiting for transfers between devices  332 us (49%)
  other arithmetic  190 us (28%)
  blocking collectives  53.2 us (8%)
  matrix products  43 us (6%)
  between operations  33.3 us (5%)
  local copies, waits for them, and re-layouts  16.9 us (3%)
    psum x2, waiting for transfers between devices, on_device(): gram_matrix = lax.psum(lax.psum(local_gram, 'chan'), 'tm')  298 us
    another operation x30, other arithmetic, on_device(): return jnp.linalg.cholesky(gram_matrix / row_total).T  172 us
    all_to_all x1, blocking collectives, on_device(): lax.all_to_all(panel, 'chan', split_axis=0, concat_axis=1, tiled=True)  53.2 us
    reduce_scatter x1, waiting for transfers between devices, on_device(): lax.psum_scatter(partial_value, 'chan', scatter_dimension=1, tiled=True)  34 us
    another operation x14, matrix products, on_device(): return jnp.linalg.cholesky(gram_matrix / row_total).T  22.9 us
    dot_general x1, matrix products, on_device(): lax.dot_general(hankel, hankel, (((0,), (0,)), ((), ())), precision=lax.P...  14.9 us
  transfers between devices with their start and end apart: 4, of which 3 were waited for; matrix products, arithmetic and copies ran while one was open for 0% of the time, Pallas kernels for 0%

profile of v1, /device:TPU:2, one launch (start us, length us, event | category | flops | bytes accessed | tf_op | source)
XLA Modules:
  0.0 670.3 jit_solution(10515232850206423874)
XLA Ops:
  6.5 5.2 convolution_bitcast_fusion
  11.8 34.0 %reduce-scatter.2.cloned.1.call-done = f32[4096,32]{0,1:T(8,128)} async-done(((f32[4096,128]{0,1:T(8,128)}), f32[4096,32]{0,1:T(8,128)}) %reduce-scatter.2.cloned.1.call-update) | async-done | bytes 524304 | tf_op jit(solution)/shard_map/reduce_scatter | solution.py:28
  45.8 1.1 broadcast_multiply_fusion.1
  46.9 1.3 collective-permute-start
  48.2 0.7 fusion.47
  67.2 53.2 %all_to_all.19 = f32[4,1024,256]{1,2,0:T(8,128)S(1)} all-to-all(f32[4,1024,256]{1,2,0:T(8,128)S(1)} %bitcast.64), channel_id=1, replica_groups=mesh['tm'=64,'chan'=4] {'chan'}, dimensions={0} | all-to-all | bytes 8388608 | tf_op jit(solution)/shard_map/all_to_all | solution.py:41
  120.4 14.9 %fusion.48 = f32[1024,1024]{0,1:T(8,128)} fusion(f32[1024,1024]{0,1:T(8,128)S(1)} %bitcast.66), kind=kOutput, calls=%fused_computation.117 | convolution fusion | flops 12884901888 | bytes 8388608 | tf_op jit(solution)/shard_map/dot_general | solution.py:43
  135.3 97.6 %all-reduce.4.cloned.1.call-done = f32[1024,1024]{0,1:T(8,128)} async-done(((f32[1024,1024]{0,1:T(8,128)}), f32[1024,1024]{0,1:T(8,128)}) %all-reduce.4.cloned.1.call-update) | async-done | bytes 4194320 | tf_op jit(solution)/shard_map/psum | solution.py:50
  233.0 200.2 %all-reduce.6.cloned.1.call-done = f32[1024,1024]{0,1:T(8,128)} async-done(((f32[1024,1024]{0,1:T(8,128)}), f32[1024,1024]{0,1:T(8,128)}) %all-reduce.6.cloned.1.call-update) | async-done | bytes 4194320 | tf_op jit(solution)/shard_map/psum | solution.py:50
  433.2 5.0 broadcast_multiply_fusion
  438.3 5.8 copy.9
  444.1 4.4 fusion
  448.6 1.9 copy-done
  450.5 11.7 %cholesky.223 = f32[128,128]{1,0:T(8,128)S(1)} custom-call(f32[128,128]{1,0:T(8,128)S(1)} %cholesky.580), custom_call_target="Cholesky" | custom-call | tf_op jit(solution)/shard_map/jit(cholesky)/cholesky | solution.py:51
  462.3 9.8 %custom-call.59 = f32[1,128,128]{1,2,0:T(8,128)S(1)} custom-call(f32[1,128,128]{2,1,0:T(8,128)S(1)} %get-tuple-element.26), custom_call_target="InvertDiagBlocksLowerTriangular" | custom-call | tf_op jit(solution)/shard_map/jit(cholesky)/cholesky | solution.py:51
  472.1 2.5 cholesky.255
  474.6 2.3 constant_dynamic-update-slice_fusion
  476.9 1.5 convolution_subtract_fusion
  478.5 11.9 %cholesky.244 = f32[128,128]{1,0:T(8,128)S(1)} custom-call(f32[128,128]{1,0:T(8,128)S(1)} %cholesky.584), custom_call_target="Cholesky" | custom-call | tf_op jit(solution)/shard_map/jit(cholesky)/cholesky | solution.py:51
  491.0 9.8 %custom-call.60 = f32[1,128,128]{1,2,0:T(8,128)S(1)} custom-call(f32[1,128,128]{2,1,0:T(8,128)S(1)} %get-tuple-element.23), custom_call_target="InvertDiagBlocksLowerTriangular" | custom-call | tf_op jit(solution)/shard_map/jit(cholesky)/cholesky | solution.py:51
  500.8 1.2 convolution_dynamic-update-slice_fusion
  502.0 2.1 convolution_subtract_fusion.1
  504.1 11.7 %cholesky.468 = f32[128,128]{1,0:T(8,128)S(1)} custom-call(f32[128,128]{1,0:T(8,128)S(1)} %cholesky.589), custom_call_target="Cholesky" | custom-call | tf_op jit(solution)/shard_map/jit(cholesky)/cholesky | solution.py:51
  517.1 9.8 %custom-call.61 = f32[1,128,128]{1,2,0:T(8,128)S(1)} custom-call(f32[1,128,128]{2,1,0:T(8,128)S(1)} %get-tuple-element.20), custom_call_target="InvertDiagBlocksLowerTriangular" | custom-call | tf_op jit(solution)/shard_map/jit(cholesky)/cholesky | solution.py:51
  526.9 1.1 convolution_dynamic-update-slice_fusion.1
  528.1 2.3 convolution_subtract_fusion.2
  530.4 11.9 %cholesky.487 = f32[128,128]{1,0:T(8,128)S(1)} custom-call(f32[128,128]{1,0:T(8,128)S(1)} %cholesky.594), custom_call_target="Cholesky" | custom-call | tf_op jit(solution)/shard_map/jit(cholesky)/cholesky | solution.py:51
  543.0 0.7 compare_reduce_fusion.4
  543.7 9.8 %custom-call.62 = f32[1,128,128]{1,2,0:T(8,128)S(1)} custom-call(f32[1,128,128]{2,1,0:T(8,128)S(1)} %get-tuple-element.17), custom_call_target="InvertDiagBlocksLowerTriangular" | custom-call | tf_op jit(solution)/shard_map/jit(cholesky)/cholesky | solution.py:51
  553.5 1.1 convolution_dynamic-update-slice_fusion.2
  554.5 2.4 convolution_subtract_fusion.3
  556.9 11.7 %cholesky.506 = f32[128,128]{1,0:T(8,128)S(1)} custom-call(f32[128,128]{1,0:T(8,128)S(1)} %cholesky.599), custom_call_target="Cholesky" | custom-call | tf_op jit(solution)/shard_map/jit(cholesky)/cholesky | solution.py:51
  569.3 0.7 compare_reduce_fusion.3
  570.0 10.2 %custom-call.63 = f32[1,128,128]{1,2,0:T(8,128)S(1)} custom-call(f32[1,128,128]{2,1,0:T(8,128)S(1)} %get-tuple-element.14), custom_call_target="InvertDiagBlocksLowerTriangular" | custom-call | tf_op jit(solution)/shard_map/jit(cholesky)/cholesky | solution.py:51
  580.2 1.0 convolution_dynamic-update-slice_fusion.3
  581.2 2.3 convolution_subtract_fusion.4
  583.5 11.7 %cholesky.526 = f32[128,128]{1,0:T(8,128)S(1)} custom-call(f32[128,128]{1,0:T(8,128)S(1)} %cholesky.604), custom_call_target="Cholesky" | custom-call | tf_op jit(solution)/shard_map/jit(cholesky)/cholesky | solution.py:51
  596.5 9.8 %custom-call.64 = f32[1,128,128]{1,2,0:T(8,128)S(1)} custom-call(f32[1,128,128]{2,1,0:T(8,128)S(1)} %get-tuple-element.11), custom_call_target="InvertDiagBlocksLowerTriangular" | custom-call | tf_op jit(solution)/shard_map/jit(cholesky)/cholesky | solution.py:51
  606.3 0.9 convolution_dynamic-update-slice_fusion.4
  607.2 2.0 convolution_subtract_fusion.5
  609.2 11.9 %cholesky.546 = f32[128,128]{1,0:T(8,128)S(1)} custom-call(f32[128,128]{1,0:T(8,128)S(1)} %cholesky.609), custom_call_target="Cholesky" | custom-call | tf_op jit(solution)/shard_map/jit(cholesky)/cholesky | solution.py:51
  622.4 9.8 %custom-call.65 = f32[1,128,128]{1,2,0:T(8,128)S(1)} custom-call(f32[1,128,128]{2,1,0:T(8,128)S(1)} %get-tuple-element.8), custom_call_target="InvertDiagBlocksLowerTriangular" | custom-call | tf_op jit(solution)/shard_map/jit(cholesky)/cholesky | solution.py:51
  632.2 0.8 convolution_dynamic-update-slice_fusion.5
  633.0 1.8 convolution_subtract_fusion.6
  634.8 11.7 %cholesky.564 = f32[128,128]{1,0:T(8,128)S(1)} custom-call(f32[128,128]{1,0:T(8,128)S(1)} %convolution_subtract_fusion.6), custom_call_target="Cholesky" | custom-call | tf_op jit(solution)/shard_map/jit(cholesky)/cholesky | solution.py:51
  647.2 0.7 compare_reduce_fusion
  653.5 4.8 select_bitcast_fusion
  658.3 5.3 copy.10
  (39 shorter events, 10.6 us)
Async XLA Ops:
  6.5 41.7 %copy-start.1 = (s32[8]{0:T(128)S(1)}, s32[8]{0:T(128)}, u32[]{:S(2)}) copy-start(s32[8]{0:T(128)} %param.5) | copy-start | bytes 100
  6.5 39.3 %reduce-scatter.2.cloned.1.call-start = ((), (), s32[]{:S(2)}) async-start(), calls=%async_computation.2 | async-start | bytes 2621440 | tf_op jit(solution)/shard_map/reduce_scatter | solution.py:28
  11.7 221.2 %all-reduce.4.cloned.1.call-start = ((), (), s32[]{:S(2)}) async-start(), calls=%async_computation.3 | async-start | bytes 8388608 | tf_op jit(solution)/shard_map/psum | solution.py:50
  46.9 16.8 %collective-permute-start = (f32[512,32]{0,1:T(8,128)S(1)}, f32[512,32]{0,1:T(8,128)S(1)}, u32[]{:S(2)}, u32[]{:S(2)}) collective-permute-start(f32[512,32]{0,1:T(8,128)S(1)} %slice.213), channel_id=1, source_target_pairs={{4,0},{8,4},{12,8},{16,12},{20,16},{24,20},{28,24},{32,28},{36,32}... | collective-permute-start | bytes 196616 | tf_op jit(solution)/shard_map/ppermute | solution.py:15
  135.3 297.9 %all-reduce.6.cloned.1.call-start = ((), (), s32[]{:S(2)}) async-start(), calls=%async_computation.4 | async-start | bytes 8388608 | tf_op jit(solution)/shard_map/psum | solution.py:50
  448.6 1.9 copy-start
Sparse Core Ops, SparseCore 0:
  11.9 33.9 reduce-scatter.1
  135.4 97.4 all-reduce.3
  236.5 196.6 all-reduce.5
